TPU v7x, 256 devices: a whole 4x4x8 slice. The times are simulated.
256 devices in a mesh: range: 8 (over y, core), radial: 32 (over x, z).
Axes of the slice: x: 4, y: 4, z: 8, core: 2. Of those that a mesh axis runs over, the one named last changes fastest.
Arguments:
- field_start: bfloat16 [2, 2048, 1024], P(None, 'radial'), may hold values from -6 to 6
- phase_table: float32 [16, 1024], replicated, may hold values from -1.5 to 1.5
- profile_index: int32 [8, 2], replicated, may hold values from 0 to 15
- group_power: float32 [4], replicated, may hold values from 0.3 to 3
- group_slot: int32 [4], replicated, may hold values from 0 to 3, each once
- source_shift: int32 [8, 32], P('range'), may hold values from 0 to 31
- slot_sub: int32 [8, 32, 16], P('range'), may hold values from 0 to 3
- tile_count: int32 [8, 32], P('range'), may hold values from 1 to 16, as said below
- row_weights: bfloat16 [8, 32, 16, 16, 256], P('range', 'radial'), may hold values from -0.375 to 0.375
- col_weights: bfloat16 [8, 32, 16, 256, 256], P('range', 'radial'), may hold values from -0.375 to 0.375
Outputs:
- interference: float32 [8, 32, 256, 256], P('range', 'radial')
Inputs may be any that keep to these rules, and one draw needn't show every extreme that they name: `tile_count`: in every slab some tile uses all 16 slots.
All inputs are finite; a program needn't handle non-finite values.
Results may differ from a plain program's by a relative error of at most 0.04.
Values may be sent and summed in bfloat16 or wider, within the bound.
A program may use at most 64 MiB of HBM per device.

v0:
```python
import math

import jax
import jax.numpy as jnp
from jax import lax
from jax.sharding import PartitionSpec as P

VB = 128
SUB = 16
K_MAX = 16
CAP = 2
GROUP_RADIALS = 512


spread_angle = 6.0
absorb_rate = 0.5


def passed_along(value, axis, steps):
    count = lax.axis_size(axis)
    leading, last = (max(0, -steps), min(count, count - steps))
    return lax.ppermute(value, axis, [(source, source + steps) for source in range(leading, last)])


def dft_tables(height):
    block_rows = height // 8
    column_ids = jnp.arange(height, dtype=jnp.int32)
    factor = 1.0 / math.sqrt(height)

    def table_block(block_index):
        row_ids = block_index * block_rows + jnp.arange(block_rows, dtype=jnp.int32)
        product = row_ids[:, None] * column_ids[None, :] % height
        angle = 2.0 * math.pi / height * product.astype(jnp.float32)
        return (
            (jnp.cos(angle) * factor).astype(jnp.bfloat16),
            (jnp.sin(angle) * factor).astype(jnp.bfloat16),
        )

    cos_blocks, sin_blocks = lax.map(table_block, jnp.arange(8, dtype=jnp.int32))
    return (cos_blocks.reshape(height, height), sin_blocks.reshape(height, height))


def spectral_phase(height):
    index_row = jnp.arange(height, dtype=jnp.int32)
    folded = jnp.minimum(index_row, height - index_row).astype(jnp.float32)
    theta = -spread_angle * (2.0 * folded / height) ** 2
    return (jnp.cos(theta), jnp.sin(theta))


def absorber_profile(height):
    level = jnp.arange(height, dtype=jnp.int32).astype(jnp.float32)
    depth = jnp.maximum(0.0, (level - 0.9375 * height) / (0.0625 * height))
    return jnp.exp(-absorb_rate * depth * depth)


def march_slab(
    field, radial_gain, phases, cosine_table, sine_table, spectral_cos, spectral_sin, absorber, band
):
    real_part = field[0]
    imag_part = field[1]
    row_total = real_part.shape[0]
    bands = []
    for step_index in range(phases.shape[0]):
        phase_cos = jnp.cos(phases[step_index])
        phase_sin = jnp.sin(phases[step_index])
        real_wide = real_part.astype(jnp.float32)
        imag_wide = imag_part.astype(jnp.float32)
        screened = jnp.concatenate(
            [
                real_wide * phase_cos - imag_wide * phase_sin,
                real_wide * phase_sin + imag_wide * phase_cos,
            ],
            0,
        ).astype(jnp.bfloat16)
        with_cos = jnp.dot(screened, cosine_table, preferred_element_type=jnp.float32)
        with_sin = jnp.dot(screened, sine_table, preferred_element_type=jnp.float32)
        spec_real = with_cos[:row_total] + with_sin[row_total:]
        spec_imag = with_cos[row_total:] - with_sin[:row_total]
        moved = jnp.concatenate(
            [
                spec_real * spectral_cos - spec_imag * spectral_sin,
                spec_real * spectral_sin + spec_imag * spectral_cos,
            ],
            0,
        ).astype(jnp.bfloat16)
        back_cos = jnp.dot(moved, cosine_table, preferred_element_type=jnp.float32)
        back_sin = jnp.dot(moved, sine_table, preferred_element_type=jnp.float32)
        real_part = ((back_cos[:row_total] - back_sin[row_total:]) * absorber).astype(jnp.bfloat16)
        imag_part = ((back_cos[row_total:] + back_sin[:row_total]) * absorber).astype(jnp.bfloat16)
        real_low = real_part.astype(jnp.float32)[:, :band]
        imag_low = imag_part.astype(jnp.float32)[:, :band]
        bands.append(
            (radial_gain[:, None] * (real_low * real_low + imag_low * imag_low)).astype(
                jnp.bfloat16
            )
        )
    return (jnp.stack([real_part, imag_part]), jnp.concatenate(bands, axis=1))


def per_device(
    field_start,
    phase_table,
    profile_index,
    group_power,
    group_slot,
    source_shift,
    slot_sub,
    tile_count,
    row_weights,
    col_weights,
):
    radial_size = lax.axis_size("radial")
    range_size = lax.axis_size("range")
    slab_index = lax.axis_index("range")
    radial_index = lax.axis_index("radial")
    height = field_start.shape[2]
    local_rows = field_start.shape[1]
    group_total = group_power.shape[0]
    cosine_table, sine_table = dft_tables(height)
    spectral_cos, spectral_sin = spectral_phase(height)
    absorber = absorber_profile(height)
    profile_count = phase_table.shape[0]
    selector = (
        profile_index[:, :, None, None]
        == jnp.arange(profile_count, dtype=jnp.int32)[None, None, :, None]
    )
    all_phases = jnp.sum(
        jnp.where(
            selector, phase_table[None, None, :, :], jnp.zeros_like(phase_table)[None, None, :, :]
        ),
        axis=2,
    )
    global_radial = radial_index * local_rows + jnp.arange(local_rows, dtype=jnp.int32)
    group_place = global_radial // GROUP_RADIALS
    group_range = jnp.arange(group_total, dtype=jnp.int32)
    group_ids = jnp.sum(
        jnp.where(group_place[:, None] == group_range[None, :], group_slot[None, :], 0), axis=1
    )
    radial_gain = jnp.sum(
        jnp.where(
            group_ids[:, None] == group_range[None, :],
            group_power[None, :],
            jnp.zeros_like(group_power)[None, :],
        ),
        axis=1,
    )
    channels = all_phases.shape[1] * VB
    phases = lax.dynamic_index_in_dim(all_phases, slab_index, 0, keepdims=False)
    batch_count = 2
    batch_rows = local_rows // batch_count

    def one_turn(turn_index, carry):
        last_field, polar_now = carry
        incoming = passed_along(last_field, "range", 1)
        batch_index = turn_index - slab_index
        active = (batch_index >= 0) & (batch_index < batch_count)
        first_row = jnp.clip(batch_index, 0, batch_count - 1) * batch_rows
        initial = lax.dynamic_slice_in_dim(field_start, first_row, batch_rows, 1)
        entering = jnp.where(slab_index == 0, initial, incoming)
        batch_gain = lax.dynamic_slice_in_dim(radial_gain, first_row, batch_rows, 0)

        def advance(field_in, gain_in, polar_in):
            leaving, bands = march_slab(
                field_in,
                gain_in,
                phases,
                cosine_table,
                sine_table,
                spectral_cos,
                spectral_sin,
                absorber,
                VB,
            )
            return (leaving, lax.dynamic_update_slice_in_dim(polar_in, bands, first_row, 0))

        def remain(field_in, gain_in, polar_in):
            return (jnp.zeros_like(field_in), polar_in)

        return lax.cond(active, advance, remain, entering, batch_gain, polar_now)

    start_field = jnp.zeros((2, batch_rows, height), jnp.bfloat16)
    polar_start = jnp.zeros((local_rows, channels), jnp.bfloat16)
    last_field, polar = lax.fori_loop(
        0, batch_count + range_size - 1, one_turn, (start_field, polar_start)
    )
    slot_ids = jnp.arange(K_MAX, dtype=jnp.int32)
    own_shift = source_shift[0, radial_index]
    own_count = tile_count[0, radial_index]
    own_subs = slot_sub[0, radial_index]
    source = (radial_index + own_shift + slot_ids // CAP) % radial_size
    every_block = lax.all_gather(polar, "radial", axis=0, tiled=True)
    row_index = (
        source[:, None] * local_rows
        + own_subs[:, None] * SUB
        + jnp.arange(SUB, dtype=jnp.int32)[None, :]
    )
    pieces = every_block[row_index]
    is_live = slot_ids < own_count
    pieces = jnp.where(is_live[:, None, None], pieces, jnp.zeros_like(pieces))
    mixed = jnp.einsum(
        "ksc,kcp->ksp", pieces, col_weights[0, 0], preferred_element_type=jnp.float32
    ).astype(jnp.bfloat16)
    tile_value = jnp.einsum(
        "ksp,ksq->pq", row_weights[0, 0], mixed, preferred_element_type=jnp.float32
    )
    return tile_value.reshape(1, 1, tile_value.shape[0], tile_value.shape[1])


def solution(mesh):
    return jax.shard_map(
        per_device,
        mesh=mesh,
        in_specs=(
            P(None, "radial", None),
            P(),
            P(),
            P(),
            P(),
            P("range", None),
            P("range", None, None),
            P("range", None),
            P("range", "radial", None, None, None),
            P("range", "radial", None, None, None),
        ),
        out_specs=P("range", "radial", None, None),
        check_vma=False,
    )
```

profile of v0, /device:TPU:24, one launch (start us, length us, event | category | flops | bytes accessed | tf_op | source)
XLA Modules:
  0.0 245.5 jit_solution(5155946689957858898)
XLA Ops:
  7.6 36.2 %while.36 = (s32[]{:T(128)}, bf16[8,128,1024]{2,1,0:T(8,128)(2,1)}, bf16[8,128,1024]{2,1,0:T(8,128)(2,1)}, s32[8]{0:T(128)S(1)}, s32[]{:T(128)}, /*index=5*/s32[1]{0:T(128)}) while((s32[]{:T(128)}, bf16[8,128,1024]{2,1,0:T(8,128)(2,1)}, bf16[8,128,1024]{2,1,0:T(8,128)(2,1)}, s32[8]{0:T(128)S(1)}, s32[]{:T(128)}, ...), condition=%wide.region_4.5_spmd.clone, body=%wide.region_3.4_spmd.clone.sunk | while | flops 2359427 | bytes 525921 | solution.py:39
  9.0 3.2 %fusion.86 = (bf16[8,128,1024]{2,1,0:T(8,128)(2,1)}, bf16[8,128,1024]{2,1,0:T(8,128)(2,1)}) fusion(bf16[8,128,1024]{2,1,0:T(8,128)(2,1)} %get-tuple-element.828, s32[]{:T(128)} %get-tuple-element.826, s32[128]{0:T(128)S(1)} %iota_add_fusion.2, bf16[8,128,1024]{2,1,0:T(8,128)(2,1)} %get-tuple-element.827), kind=kLoop, calls=%fused_computation.18.clone.1 | loop fusion | flops 2359296 | bytes 525312 | tf_op jit(solution)/shard_map/while/body/jit(dynamic_update_index_in_dim)/dynamic_update_slice | solution.py:39
  13.5 3.2 %fusion.86 = (bf16[8,128,1024]{2,1,0:T(8,128)(2,1)}, bf16[8,128,1024]{2,1,0:T(8,128)(2,1)}) fusion(bf16[8,128,1024]{2,1,0:T(8,128)(2,1)} %get-tuple-element.828, s32[]{:T(128)} %get-tuple-element.826, s32[128]{0:T(128)S(1)} %iota_add_fusion.2, bf16[8,128,1024]{2,1,0:T(8,128)(2,1)} %get-tuple-element.827), kind=kLoop, calls=%fused_computation.18.clone.1 | loop fusion | flops 2359296 | bytes 525312 | tf_op jit(solution)/shard_map/while/body/jit(dynamic_update_index_in_dim)/dynamic_update_slice | solution.py:39
  18.0 3.2 %fusion.86 = (bf16[8,128,1024]{2,1,0:T(8,128)(2,1)}, bf16[8,128,1024]{2,1,0:T(8,128)(2,1)}) fusion(bf16[8,128,1024]{2,1,0:T(8,128)(2,1)} %get-tuple-element.828, s32[]{:T(128)} %get-tuple-element.826, s32[128]{0:T(128)S(1)} %iota_add_fusion.2, bf16[8,128,1024]{2,1,0:T(8,128)(2,1)} %get-tuple-element.827), kind=kLoop, calls=%fused_computation.18.clone.1 | loop fusion | flops 2359296 | bytes 525312 | tf_op jit(solution)/shard_map/while/body/jit(dynamic_update_index_in_dim)/dynamic_update_slice | solution.py:39
  22.5 3.2 %fusion.86 = (bf16[8,128,1024]{2,1,0:T(8,128)(2,1)}, bf16[8,128,1024]{2,1,0:T(8,128)(2,1)}) fusion(bf16[8,128,1024]{2,1,0:T(8,128)(2,1)} %get-tuple-element.828, s32[]{:T(128)} %get-tuple-element.826, s32[128]{0:T(128)S(1)} %iota_add_fusion.2, bf16[8,128,1024]{2,1,0:T(8,128)(2,1)} %get-tuple-element.827), kind=kLoop, calls=%fused_computation.18.clone.1 | loop fusion | flops 2359296 | bytes 525312 | tf_op jit(solution)/shard_map/while/body/jit(dynamic_update_index_in_dim)/dynamic_update_slice | solution.py:39
  27.0 3.2 %fusion.86 = (bf16[8,128,1024]{2,1,0:T(8,128)(2,1)}, bf16[8,128,1024]{2,1,0:T(8,128)(2,1)}) fusion(bf16[8,128,1024]{2,1,0:T(8,128)(2,1)} %get-tuple-element.828, s32[]{:T(128)} %get-tuple-element.826, s32[128]{0:T(128)S(1)} %iota_add_fusion.2, bf16[8,128,1024]{2,1,0:T(8,128)(2,1)} %get-tuple-element.827), kind=kLoop, calls=%fused_computation.18.clone.1 | loop fusion | flops 2359296 | bytes 525312 | tf_op jit(solution)/shard_map/while/body/jit(dynamic_update_index_in_dim)/dynamic_update_slice | solution.py:39
  31.5 3.2 %fusion.86 = (bf16[8,128,1024]{2,1,0:T(8,128)(2,1)}, bf16[8,128,1024]{2,1,0:T(8,128)(2,1)}) fusion(bf16[8,128,1024]{2,1,0:T(8,128)(2,1)} %get-tuple-element.828, s32[]{:T(128)} %get-tuple-element.826, s32[128]{0:T(128)S(1)} %iota_add_fusion.2, bf16[8,128,1024]{2,1,0:T(8,128)(2,1)} %get-tuple-element.827), kind=kLoop, calls=%fused_computation.18.clone.1 | loop fusion | flops 2359296 | bytes 525312 | tf_op jit(solution)/shard_map/while/body/jit(dynamic_update_index_in_dim)/dynamic_update_slice | solution.py:39
  36.1 3.2 %fusion.86 = (bf16[8,128,1024]{2,1,0:T(8,128)(2,1)}, bf16[8,128,1024]{2,1,0:T(8,128)(2,1)}) fusion(bf16[8,128,1024]{2,1,0:T(8,128)(2,1)} %get-tuple-element.828, s32[]{:T(128)} %get-tuple-element.826, s32[128]{0:T(128)S(1)} %iota_add_fusion.2, bf16[8,128,1024]{2,1,0:T(8,128)(2,1)} %get-tuple-element.827), kind=kLoop, calls=%fused_computation.18.clone.1 | loop fusion | flops 2359296 | bytes 525312 | tf_op jit(solution)/shard_map/while/body/jit(dynamic_update_index_in_dim)/dynamic_update_slice | solution.py:39
  40.6 3.2 %fusion.86 = (bf16[8,128,1024]{2,1,0:T(8,128)(2,1)}, bf16[8,128,1024]{2,1,0:T(8,128)(2,1)}) fusion(bf16[8,128,1024]{2,1,0:T(8,128)(2,1)} %get-tuple-element.828, s32[]{:T(128)} %get-tuple-element.826, s32[128]{0:T(128)S(1)} %iota_add_fusion.2, bf16[8,128,1024]{2,1,0:T(8,128)(2,1)} %get-tuple-element.827), kind=kLoop, calls=%fused_computation.18.clone.1 | loop fusion | flops 2359296 | bytes 525312 | tf_op jit(solution)/shard_map/while/body/jit(dynamic_update_index_in_dim)/dynamic_update_slice | solution.py:39
  45.0 107.3 %while.37 = (s32[]{:T(128)}, bf16[2,32,1024]{2,1,0:T(8,128)(2,1)}, bf16[64,256]{1,0:T(8,128)(2,1)S(1)}, s32[]{:T(128)}, pred[]{:T(512)}, /*index=5*/bf16[2,64,10...) while((s32[]{:T(128)}, bf16[2,32,1024]{2,1,0:T(8,128)(2,1)}, ...), condition=%wide.region_8.9_spmd.clone.clone, body=%wide.region_5.8_spmd.clone.clone.sunk | while | flops 1077768192 | bytes 41497424 | solution.py:183
  47.1 4.5 %collective-permute-done = bf16[2,32,1024]{2,1,0:T(8,128)(2,1)S(1)} collective-permute-done((bf16[2,32,1024]{2,1,0:T(8,128)(2,1)}, bf16[2,32,1024]{2,1,0:T(8,128)(2,1)S(1)}, u32[]{:S(2)}, u32[]{:S(2)}) %collective-permute-start) | collective-permute-done | bytes 131104 | tf_op jit(solution)/shard_map/while/body/eval_jaxpr/ppermute | solution.py:22
  54.3 4.5 %collective-permute-done = bf16[2,32,1024]{2,1,0:T(8,128)(2,1)S(1)} collective-permute-done((bf16[2,32,1024]{2,1,0:T(8,128)(2,1)}, bf16[2,32,1024]{2,1,0:T(8,128)(2,1)S(1)}, u32[]{:S(2)}, u32[]{:S(2)}) %collective-permute-start) | collective-permute-done | bytes 131104 | tf_op jit(solution)/shard_map/while/body/eval_jaxpr/ppermute | solution.py:22
  61.4 4.5 %collective-permute-done = bf16[2,32,1024]{2,1,0:T(8,128)(2,1)S(1)} collective-permute-done((bf16[2,32,1024]{2,1,0:T(8,128)(2,1)}, bf16[2,32,1024]{2,1,0:T(8,128)(2,1)S(1)}, u32[]{:S(2)}, u32[]{:S(2)}) %collective-permute-start) | collective-permute-done | bytes 131104 | tf_op jit(solution)/shard_map/while/body/eval_jaxpr/ppermute | solution.py:22
  68.6 4.5 %collective-permute-done = bf16[2,32,1024]{2,1,0:T(8,128)(2,1)S(1)} collective-permute-done((bf16[2,32,1024]{2,1,0:T(8,128)(2,1)}, bf16[2,32,1024]{2,1,0:T(8,128)(2,1)S(1)}, u32[]{:S(2)}, u32[]{:S(2)}) %collective-permute-start) | collective-permute-done | bytes 131104 | tf_op jit(solution)/shard_map/while/body/eval_jaxpr/ppermute | solution.py:22
  75.7 4.5 %collective-permute-done = bf16[2,32,1024]{2,1,0:T(8,128)(2,1)S(1)} collective-permute-done((bf16[2,32,1024]{2,1,0:T(8,128)(2,1)}, bf16[2,32,1024]{2,1,0:T(8,128)(2,1)S(1)}, u32[]{:S(2)}, u32[]{:S(2)}) %collective-permute-start) | collective-permute-done | bytes 131104 | tf_op jit(solution)/shard_map/while/body/eval_jaxpr/ppermute | solution.py:22
  82.9 4.5 %collective-permute-done = bf16[2,32,1024]{2,1,0:T(8,128)(2,1)S(1)} collective-permute-done((bf16[2,32,1024]{2,1,0:T(8,128)(2,1)}, bf16[2,32,1024]{2,1,0:T(8,128)(2,1)S(1)}, u32[]{:S(2)}, u32[]{:S(2)}) %collective-permute-start) | collective-permute-done | bytes 131104 | tf_op jit(solution)/shard_map/while/body/eval_jaxpr/ppermute | solution.py:22
  90.1 32.4 %collective-permute-done = bf16[2,32,1024]{2,1,0:T(8,128)(2,1)S(1)} collective-permute-done((bf16[2,32,1024]{2,1,0:T(8,128)(2,1)}, bf16[2,32,1024]{2,1,0:T(8,128)(2,1)S(1)}, u32[]{:S(2)}, u32[]{:S(2)}) %collective-permute-start) | collective-permute-done | bytes 131104 | tf_op jit(solution)/shard_map/while/body/eval_jaxpr/ppermute | solution.py:22
  122.5 8.1 %conditional.4 = (bf16[2,32,1024]{2,1,0:T(8,128)(2,1)}, bf16[64,256]{1,0:T(8,128)(2,1)S(1)}) conditional(s32[]{:T(128)} %convert_element_type.272, bf16[64,256]{1,0:T(8,128)(2,1)S(1)} %get-tuple-element.853, (pred[]{:T(512)}, s32[]{:T(128)}, bf16[2,64,1024]{2,1,0:T(8,128)(2,1)S(1)}, bf16[2,32,1024]{2,1,0:T(8,128)(2,1)S(1)}, ...), branch_computations={%region_6.6_spmd, %region_7.7_spmd.clone} | conditional | flops 1077757952 | bytes 40964636 | solution.py:179
  122.8 2.2 fusion.35
  132.5 4.5 %collective-permute-done = bf16[2,32,1024]{2,1,0:T(8,128)(2,1)S(1)} collective-permute-done((bf16[2,32,1024]{2,1,0:T(8,128)(2,1)}, bf16[2,32,1024]{2,1,0:T(8,128)(2,1)S(1)}, u32[]{:S(2)}, u32[]{:S(2)}) %collective-permute-start) | collective-permute-done | bytes 131104 | tf_op jit(solution)/shard_map/while/body/eval_jaxpr/ppermute | solution.py:22
  137.1 8.1 %conditional.4 = (bf16[2,32,1024]{2,1,0:T(8,128)(2,1)}, bf16[64,256]{1,0:T(8,128)(2,1)S(1)}) conditional(s32[]{:T(128)} %convert_element_type.272, bf16[64,256]{1,0:T(8,128)(2,1)S(1)} %get-tuple-element.853, (pred[]{:T(512)}, s32[]{:T(128)}, bf16[2,64,1024]{2,1,0:T(8,128)(2,1)S(1)}, bf16[2,32,1024]{2,1,0:T(8,128)(2,1)S(1)}, ...), branch_computations={%region_6.6_spmd, %region_7.7_spmd.clone} | conditional | flops 1077757952 | bytes 40964636 | solution.py:179
  147.1 4.5 %collective-permute-done = bf16[2,32,1024]{2,1,0:T(8,128)(2,1)S(1)} collective-permute-done((bf16[2,32,1024]{2,1,0:T(8,128)(2,1)}, bf16[2,32,1024]{2,1,0:T(8,128)(2,1)S(1)}, u32[]{:S(2)}, u32[]{:S(2)}) %collective-permute-start) | collective-permute-done | bytes 131104 | tf_op jit(solution)/shard_map/while/body/eval_jaxpr/ppermute | solution.py:22
  155.2 79.5 %all-gather.2.cloned.1.call-done = bf16[2048,256]{1,0:T(8,128)(2,1)} async-done(((bf16[64,256]{1,0:T(8,128)(2,1)}), bf16[2048,256]{1,0:T(8,128)(2,1)}) %all-gather.2.cloned.1.call-update) | async-done | bytes 1048592 | tf_op jit(solution)/shard_map/all_gather | solution.py:191
  234.8 2.3 gather_fusion
  (144 shorter events, 51.6 us)
Async XLA Ops:
  6.5 230.6 %copy-start = (bf16[1,1,16,256,256]{4,3,2,1,0:T(8,128)(2,1)S(1)}, bf16[1,1,16,256,256]{4,3,2,1,0:T(8,128)(2,1)}, u32[]{:S(2)}) copy-start(bf16[1,1,16,256,256]{4,3,2,1,0:T(8,128)(2,1)} %param.25) | copy-start | bytes 6291460
  6.5 37.3 %copy-start.6 = (f32[16,1024]{1,0:T(8,128)S(1)}, f32[16,1024]{1,0:T(8,128)}, u32[]{:S(2)}) copy-start(f32[16,1024]{1,0:T(8,128)} %param.17) | copy-start | bytes 196612
  6.5 37.6 %copy-start.10 = (s32[4]{0:T(128)S(1)}, s32[4]{0:T(128)}, u32[]{:S(2)}) copy-start(s32[4]{0:T(128)} %param.20) | copy-start | bytes 52
  6.5 37.7 %copy-start.11 = (f32[4]{0:T(128)S(1)}, f32[4]{0:T(128)}, u32[]{:S(2)}) copy-start(f32[4]{0:T(128)} %param.19) | copy-start | bytes 52
  6.5 38.5 %copy-start.3 = (bf16[2,64,1024]{2,1,0:T(8,128)(2,1)S(1)}, bf16[2,64,1024]{2,1,0:T(8,128)(2,1)}, u32[]{:S(2)}) copy-start(bf16[2,64,1024]{2,1,0:T(8,128)(2,1)} %param.16) | copy-start | bytes 786436
  6.5 228.2 %all-gather.2.cloned.1.call-start = ((), (), s32[]{:S(2)}) async-start(), calls=%async_computation | async-start | bytes 1081344 | tf_op jit(solution)/shard_map/all_gather | solution.py:191
  45.0 108.0 %copy-start.8 = (s32[1,32]{1,0:T(1,128)S(1)}, s32[1,32]{1,0:T(1,128)}, u32[]{:S(2)}) copy-start(s32[1,32]{1,0:T(1,128)} %param.21) | copy-start | bytes 388
  45.0 108.0 %copy-start.9 = (s32[1,32]{1,0:T(1,128)S(1)}, s32[1,32]{1,0:T(1,128)}, u32[]{:S(2)}) copy-start(s32[1,32]{1,0:T(1,128)} %param.23) | copy-start | bytes 388
  45.0 109.2 %copy-start.7 = (s32[1,32,16]{1,2,0:T(8,128)S(1)}, s32[1,32,16]{1,2,0:T(8,128)}, u32[]{:S(2)}) copy-start(s32[1,32,16]{1,2,0:T(8,128)} %param.22) | copy-start | bytes 6148
  45.0 192.1 %copy-start.4 = (bf16[1,1,16,16,256]{4,3,2,1,0:T(8,128)(2,1)S(1)}, bf16[1,1,16,16,256]{4,3,2,1,0:T(8,128)(2,1)}, u32[]{:S(2)}) copy-start(bf16[1,1,16,16,256]{4,3,2,1,0:T(8,128)(2,1)} %param.24) | copy-start | bytes 393220
  45.1 6.6 %collective-permute-start = (bf16[2,32,1024]{2,1,0:T(8,128)(2,1)}, bf16[2,32,1024]{2,1,0:T(8,128)(2,1)S(1)}, u32[]{:S(2)}, u32[]{:S(2)}) collective-permute-start(bf16[2,32,1024]{2,1,0:T(8,128)(2,1)} %get-tuple-element.852), channel_id=1, source_target_pairs={{0,32},{32,64},{64,96},{96,128},{128,160},{160,192},{192,224},{1,3... | collective-permute-start | bytes 393224 | tf_op jit(solution)/shard_map/while/body/eval_jaxpr/ppermute | solution.py:22
  52.4 6.5 %collective-permute-start = (bf16[2,32,1024]{2,1,0:T(8,128)(2,1)}, bf16[2,32,1024]{2,1,0:T(8,128)(2,1)S(1)}, u32[]{:S(2)}, u32[]{:S(2)}) collective-permute-start(bf16[2,32,1024]{2,1,0:T(8,128)(2,1)} %get-tuple-element.852), channel_id=1, source_target_pairs={{0,32},{32,64},{64,96},{96,128},{128,160},{160,192},{192,224},{1,3... | collective-permute-start | bytes 393224 | tf_op jit(solution)/shard_map/while/body/eval_jaxpr/ppermute | solution.py:22
  59.5 6.5 %collective-permute-start = (bf16[2,32,1024]{2,1,0:T(8,128)(2,1)}, bf16[2,32,1024]{2,1,0:T(8,128)(2,1)S(1)}, u32[]{:S(2)}, u32[]{:S(2)}) collective-permute-start(bf16[2,32,1024]{2,1,0:T(8,128)(2,1)} %get-tuple-element.852), channel_id=1, source_target_pairs={{0,32},{32,64},{64,96},{96,128},{128,160},{160,192},{192,224},{1,3... | collective-permute-start | bytes 393224 | tf_op jit(solution)/shard_map/while/body/eval_jaxpr/ppermute | solution.py:22
  66.7 6.5 %collective-permute-start = (bf16[2,32,1024]{2,1,0:T(8,128)(2,1)}, bf16[2,32,1024]{2,1,0:T(8,128)(2,1)S(1)}, u32[]{:S(2)}, u32[]{:S(2)}) collective-permute-start(bf16[2,32,1024]{2,1,0:T(8,128)(2,1)} %get-tuple-element.852), channel_id=1, source_target_pairs={{0,32},{32,64},{64,96},{96,128},{128,160},{160,192},{192,224},{1,3... | collective-permute-start | bytes 393224 | tf_op jit(solution)/shard_map/while/body/eval_jaxpr/ppermute | solution.py:22
  73.8 6.5 %collective-permute-start = (bf16[2,32,1024]{2,1,0:T(8,128)(2,1)}, bf16[2,32,1024]{2,1,0:T(8,128)(2,1)S(1)}, u32[]{:S(2)}, u32[]{:S(2)}) collective-permute-start(bf16[2,32,1024]{2,1,0:T(8,128)(2,1)} %get-tuple-element.852), channel_id=1, source_target_pairs={{0,32},{32,64},{64,96},{96,128},{128,160},{160,192},{192,224},{1,3... | collective-permute-start | bytes 393224 | tf_op jit(solution)/shard_map/while/body/eval_jaxpr/ppermute | solution.py:22
  81.0 6.5 %collective-permute-start = (bf16[2,32,1024]{2,1,0:T(8,128)(2,1)}, bf16[2,32,1024]{2,1,0:T(8,128)(2,1)S(1)}, u32[]{:S(2)}, u32[]{:S(2)}) collective-permute-start(bf16[2,32,1024]{2,1,0:T(8,128)(2,1)} %get-tuple-element.852), channel_id=1, source_target_pairs={{0,32},{32,64},{64,96},{96,128},{128,160},{160,192},{192,224},{1,3... | collective-permute-start | bytes 393224 | tf_op jit(solution)/shard_map/while/body/eval_jaxpr/ppermute | solution.py:22
  88.1 34.4 %collective-permute-start = (bf16[2,32,1024]{2,1,0:T(8,128)(2,1)}, bf16[2,32,1024]{2,1,0:T(8,128)(2,1)S(1)}, u32[]{:S(2)}, u32[]{:S(2)}) collective-permute-start(bf16[2,32,1024]{2,1,0:T(8,128)(2,1)} %get-tuple-element.852), channel_id=1, source_target_pairs={{0,32},{32,64},{64,96},{96,128},{128,160},{160,192},{192,224},{1,3... | collective-permute-start | bytes 393224 | tf_op jit(solution)/shard_map/while/body/eval_jaxpr/ppermute | solution.py:22
  122.5 2.6 %copy-start.2 = (bf16[1024,1024]{1,0:T(8,128)(2,1)S(1)}, bf16[1024,1024]{1,0:T(8,128)(2,1)}, u32[]{:S(2)}) copy-start(bf16[1024,1024]{1,0:T(8,128)(2,1)} %get-tuple-element.647) | copy-start | bytes 6291460 | tf_op jit(solution)/shard_map/while/body/eval_jaxpr/cond
  125.1 1.6 copy-start.1
  130.6 6.5 %collective-permute-start = (bf16[2,32,1024]{2,1,0:T(8,128)(2,1)}, bf16[2,32,1024]{2,1,0:T(8,128)(2,1)S(1)}, u32[]{:S(2)}, u32[]{:S(2)}) collective-permute-start(bf16[2,32,1024]{2,1,0:T(8,128)(2,1)} %get-tuple-element.852), channel_id=1, source_target_pairs={{0,32},{32,64},{64,96},{96,128},{128,160},{160,192},{192,224},{1,3... | collective-permute-start | bytes 393224 | tf_op jit(solution)/shard_map/while/body/eval_jaxpr/ppermute | solution.py:22
  137.1 2.6 %copy-start.2 = (bf16[1024,1024]{1,0:T(8,128)(2,1)S(1)}, bf16[1024,1024]{1,0:T(8,128)(2,1)}, u32[]{:S(2)}) copy-start(bf16[1024,1024]{1,0:T(8,128)(2,1)} %get-tuple-element.647) | copy-start | bytes 6291460 | tf_op jit(solution)/shard_map/while/body/eval_jaxpr/cond
  139.7 1.6 copy-start.1
  145.2 6.5 %collective-permute-start = (bf16[2,32,1024]{2,1,0:T(8,128)(2,1)}, bf16[2,32,1024]{2,1,0:T(8,128)(2,1)S(1)}, u32[]{:S(2)}, u32[]{:S(2)}) collective-permute-start(bf16[2,32,1024]{2,1,0:T(8,128)(2,1)} %get-tuple-element.852), channel_id=1, source_target_pairs={{0,32},{32,64},{64,96},{96,128},{128,160},{160,192},{192,224},{1,3... | collective-permute-start | bytes 393224 | tf_op jit(solution)/shard_map/while/body/eval_jaxpr/ppermute | solution.py:22
  152.3 0.6 copy-start.5
Sparse Core Ops, SparseCore 0:
  153.1 81.6 all-gather.1
where the time goes:
time: 246 us; the launch traced here: 245 us
  waiting for transfers between devices  148 us (60%)
  other arithmetic  29.2 us (12%)
  local copies, waits for them, and re-layouts  18.6 us (8%)
  starting transfers between devices  17.4 us (7%)
  between operations  14.1 us (6%)
  matrix products  11.8 us (5%)
  loops' own time  6.04 us (2%)
    all_gather x1, waiting for transfers between devices, per_device(): every_block = lax.all_gather(polar, 'radial', axis=0, tiled=True)  79.5 us
    ppermute x9, waiting for transfers between devices, passed_along(): lax.ppermute(value, axis, [(source, source + steps) for source in range(l...  68.8 us
    dynamic_update_slice x8, other arithmetic, dft_tables(): lax.map(table_block, jnp.arange(8, dtype=jnp.int32))  25.5 us
    ppermute x9, starting transfers between devices, passed_along(): lax.ppermute(value, axis, [(source, source + steps) for source in range(l...  17.3 us
    another operation x1, loops' own time, dft_tables(): lax.map(table_block, jnp.arange(8, dtype=jnp.int32))  5.51 us
    dot_general x4, matrix products, march_slab(): jnp.dot(screened, cosine_table, preferred_element_type=jnp.float32)  5.42 us
    another operation x8, local copies, waits for them, and re-layouts  5.33 us
    dynamic_slice x8, local copies, waits for them, and re-layouts, dft_tables(): lax.map(table_block, jnp.arange(8, dtype=jnp.int32))  5.17 us
  transfers between devices with their start and end apart: 10, of which 10 were waited for; matrix products, arithmetic and copies ran while one was open for 1% of the time, Pallas kernels for 0%

commit v1 on v0

v1 whole, which is shorter than its diff:
```python
import functools

import jax
import jax.numpy as jnp
import ml_dtypes
import numpy as np
from jax import lax
from jax.experimental import pallas as pl
from jax.experimental.pallas import tpu as pltpu
from jax.sharding import PartitionSpec as P

MESH = pl.DeviceIdType.MESH
F32 = jnp.float32
BF16 = jnp.bfloat16

H = 1024
CHUNK = 256
VB = 128
SUB = 16
PIX = 256
K_MAX = 16
SLABS = 8
NX = 4
NZ = 8
GROUP_DEVICES = 8

spread_angle = 6.0
absorb_rate = 0.5


def propagator_blocks():
    order = np.arange(H)
    folded = np.minimum(order, H - order)
    theta = -spread_angle * (2.0 * folded / H) ** 2
    lagged = np.fft.ifft(np.exp(1j * theta))
    place = np.arange(CHUNK)
    lag = place[None, :] - place[:, None]
    turn = (1.0, -1j, -1.0, 1j)
    blocks = []
    for j in range(4):
        block = sum(turn[j * c % 4] * lagged[(CHUNK * c + lag) % H] for c in range(4)) / 4
        blocks.append(np.concatenate([block.real, block.imag], axis=1))
    return np.stack(blocks).astype(ml_dtypes.bfloat16)


def absorber_tail():
    level = np.arange(H - 128, H)
    depth = np.maximum(0.0, (level - 0.9375 * H) / (0.0625 * H))
    return np.exp(-absorb_rate * depth * depth).astype(np.float32).reshape(1, 128)


def cos_sin(angle):
    sq = angle * angle
    cosine = F32(-1.0 / 87178291200)
    for value in (1.0 / 479001600, -1.0 / 3628800, 1.0 / 40320, -1.0 / 720, 1.0 / 24, -1.0 / 2, 1.0):
        cosine = cosine * sq + F32(value)
    sine = F32(1.0 / 6227020800)
    for value in (-1.0 / 39916800, 1.0 / 362880, -1.0 / 5040, 1.0 / 120, -1.0 / 6, 1.0):
        sine = sine * sq + F32(value)
    return cosine, sine * angle


def kernel(
    field_hbm,
    phase_hbm,
    profile_hbm,
    power_hbm,
    slot_hbm,
    shift_hbm,
    sub_hbm,
    count_hbm,
    row_hbm,
    col_hbm,
    block_hbm,
    tail_hbm,
    out_ref,
    field_in,
    phase_in,
    cos_tab,
    sin_tab,
    blocks,
    tail,
    row_in,
    col_in,
    march,
    sent,
    gathered,
    picked,
    landed,
    row_turned,
    mixed,
    profile,
    power,
    slot,
    shift,
    sub_of,
    count,
    in_sem,
    send_sem,
    recv_sem,
    send2_sem,
    recv2_sem,
):
    n_own = lax.axis_index("range")
    r_own = lax.axis_index("radial")
    pair = n_own // 4
    part = n_own % 4
    x_own = r_own // NZ
    z_own = r_own % NZ

    first_row = pl.multiple_of(part * SUB, SUB)
    loads = [
        pltpu.make_async_copy(field_hbm.at[:, pl.ds(first_row, SUB), :], field_in, in_sem.at[0]),
        pltpu.make_async_copy(phase_hbm, phase_in, in_sem.at[1]),
        pltpu.make_async_copy(profile_hbm, profile, in_sem.at[2]),
        pltpu.make_async_copy(power_hbm, power, in_sem.at[3]),
        pltpu.make_async_copy(slot_hbm, slot, in_sem.at[4]),
        pltpu.make_async_copy(block_hbm, blocks, in_sem.at[5]),
        pltpu.make_async_copy(tail_hbm, tail, in_sem.at[6]),
        pltpu.make_async_copy(shift_hbm, shift, in_sem.at[7]),
        pltpu.make_async_copy(sub_hbm, sub_of, in_sem.at[8]),
        pltpu.make_async_copy(count_hbm, count, in_sem.at[9]),
        pltpu.make_async_copy(row_hbm.at[0, 0], row_in, in_sem.at[10]),
        pltpu.make_async_copy(col_hbm.at[0, 0], col_in, in_sem.at[11]),
    ]
    for load in loads:
        load.start()

    barrier = pltpu.get_barrier_semaphore()
    for dp in range(4):
        for dx in range(NX):
            if dp or dx:
                peer = (pair * 4 + (part + dp) % 4, (x_own + dx) % NX * NZ + z_own)
                pl.semaphore_signal(barrier, inc=1, device_id=peer, device_id_type=MESH)
    for dz in range(1, NZ):
        peer = (n_own, x_own * NZ + (z_own + dz) % NZ)
        pl.semaphore_signal(barrier, inc=1, device_id=peer, device_id_type=MESH)

    for load in loads[:7]:
        load.wait()
    cosine, sine = cos_sin(phase_in[...])
    cos_tab[...] = cosine
    sin_tab[...] = sine
    march[...] = field_in[...].astype(F32)
    gain = power[slot[x_own // (GROUP_DEVICES // NZ)]]

    def one_step(re, im, number, step):
        row = profile[number, step]
        cosine = cos_tab[pl.ds(row, 1), :]
        sine = sin_tab[pl.ds(row, 1), :]
        sr = re * cosine - im * sine
        si = re * sine + im * cosine
        r0, r1, r2, r3 = (sr[:, a * CHUNK : (a + 1) * CHUNK] for a in range(4))
        i0, i1, i2, i3 = (si[:, a * CHUNK : (a + 1) * CHUNK] for a in range(4))
        er, ei, fr, fi = r0 + r2, i0 + i2, r1 + r3, i1 + i3
        gr, gi, hr, hi = r0 - r2, i0 - i2, r1 - r3, i1 - i3
        entering = ((er + fr, ei + fi), (gr + hi, gi - hr), (er - fr, ei - fi), (gr - hi, gi + hr))
        leaving = []
        for j, (vr, vi) in enumerate(entering):
            both = jnp.concatenate([vr, vi], axis=0).astype(BF16)
            product = jnp.dot(both, blocks[j], preferred_element_type=F32)
            leaving.append(
                (
                    product[:SUB, :CHUNK] - product[SUB:, CHUNK:],
                    product[:SUB, CHUNK:] + product[SUB:, :CHUNK],
                )
            )
        (y0r, y0i), (y1r, y1i), (y2r, y2i), (y3r, y3i) = leaving
        pr, pi, qr, qi = y0r + y2r, y0i + y2i, y0r - y2r, y0i - y2i
        tr, ti, dr, di = y1r + y3r, y1i + y3i, y1r - y3r, y1i - y3i
        re = jnp.concatenate([pr + tr, qr - di, pr - tr, qr + di], axis=1)
        im = jnp.concatenate([pi + ti, qi + dr, pi - ti, qi - dr], axis=1)
        top = tail[...]
        re = jnp.concatenate([re[:, : H - 128], re[:, H - 128 :] * top], axis=1)
        im = jnp.concatenate([im[:, : H - 128], im[:, H - 128 :] * top], axis=1)
        return re, im

    def warm(number, carry):
        re, im = march[0], march[1]
        for step in range(2):
            re, im = one_step(re, im, number, step)
        march[0] = re
        march[1] = im
        return carry

    lax.fori_loop(0, pair * 4, warm, 0)

    pl.semaphore_wait(barrier, 4 * NX - 1 + NZ - 1)

    def block_copy(j, dx):
        return pltpu.make_async_remote_copy(
            src_ref=sent.at[j],
            dst_ref=gathered.at[x_own, part],
            send_sem=send_sem.at[j, dx],
            recv_sem=recv_sem.at[x_own, part],
            device_id=(pair * 4 + j, (x_own + dx) % NX * NZ + z_own),
            device_id_type=MESH,
        )

    def live(j, carry):
        re, im = march[0], march[1]
        bands = []
        for step in range(2):
            re, im = one_step(re, im, pair * 4 + j, step)
            low_re, low_im = re[:, :VB], im[:, :VB]
            bands.append(gain * (low_re * low_re + low_im * low_im))
        polar = jnp.concatenate(bands, axis=1).astype(BF16)
        sent[j] = polar

        @pl.when(j == part)
        def _():
            gathered[x_own, part] = polar

        march[0] = re
        march[1] = im
        for dx in range(1, NX):
            block_copy(j, dx).start()

        @pl.when(j != part)
        def _():
            block_copy(j, 0).start()

        return carry

    lax.fori_loop(0, 4, live, 0)

    for load in loads[7:]:
        load.wait()
    own_shift = shift[0, r_own]

    def slot_pair(dz):
        return lax.rem(2 * NZ - dz + NZ * 4 - own_shift, NZ)

    rows = []
    for dz in range(NZ):
        first = 2 * slot_pair(dz)
        rows.append(row_in[first])
        rows.append(row_in[first + 1])
    row_turned[...] = jnp.concatenate(rows, axis=0).T

    def arrived(xs, ps):
        return pltpu.make_async_remote_copy(
            src_ref=sent.at[0],
            dst_ref=gathered.at[xs, ps],
            send_sem=send_sem.at[0, 0],
            recv_sem=recv_sem.at[xs, ps],
            device_id=(n_own, r_own),
            device_id_type=MESH,
        )

    for dp in range(4):
        for dx in range(NX):
            if dp or dx:
                arrived((x_own + dx) % NX, (part + dp) % 4).wait_recv()

    def pick_copy(dz):
        return pltpu.make_async_remote_copy(
            src_ref=picked.at[dz],
            dst_ref=landed.at[dz],
            send_sem=send2_sem.at[dz],
            recv_sem=recv2_sem.at[dz],
            device_id=(n_own, x_own * NZ + (z_own + dz) % NZ),
            device_id_type=MESH,
        )

    for dz in (4, 3, 5, 2, 6, 1, 7, 0):
        tile = x_own * NZ + (z_own + dz) % NZ
        begin = tile + shift[0, tile]
        ahead = lax.rem(z_own + 64 - lax.rem(begin, NZ), NZ)
        source = lax.rem(lax.rem(begin + ahead, NX * NZ) // NZ, NX)
        for i in range(2):
            k = 2 * ahead + i
            block = gathered[source, sub_of[0, tile, k]]
            block = jnp.where(k < count[0, tile], block, jnp.zeros_like(block))
            if dz:
                picked[dz, i] = block
            else:
                landed[0, i] = block
        if dz:
            pick_copy(dz).start()

    for dz in (0, 1, 7, 2, 6, 3, 5, 4):
        if dz:
            pick_copy(dz).wait_recv()
        first = 2 * slot_pair(dz)
        for i in range(2):
            product = jnp.dot(landed[dz, i], col_in[first + i], preferred_element_type=F32)
            mixed[dz * 2 * SUB + i * SUB : dz * 2 * SUB + (i + 1) * SUB, :] = product.astype(BF16)
    out_ref[0, 0] = jnp.dot(row_turned[...], mixed[...], preferred_element_type=F32)

    def sends_done(j, carry):
        for dx in range(1, NX):
            block_copy(j, dx).wait_send()

        @pl.when(j != part)
        def _():
            block_copy(j, 0).wait_send()

        return carry

    lax.fori_loop(0, 4, sends_done, 0)
    for dz in range(1, NZ):
        pick_copy(dz).wait_send()


def per_device(
    field_start,
    phase_table,
    profile_index,
    group_power,
    group_slot,
    source_shift,
    slot_sub,
    tile_count,
    row_weights,
    col_weights,
):
    dma = pltpu.SemaphoreType.DMA
    anywhere = pl.BlockSpec(memory_space=pl.ANY)
    return pl.pallas_call(
        kernel,
        out_shape=jax.ShapeDtypeStruct((1, 1, PIX, PIX), F32),
        in_specs=[anywhere] * 12,
        out_specs=pl.BlockSpec(memory_space=pltpu.VMEM),
        scratch_shapes=[
            pltpu.VMEM((2, SUB, H), BF16),
            pltpu.VMEM(phase_table.shape, F32),
            pltpu.VMEM(phase_table.shape, F32),
            pltpu.VMEM(phase_table.shape, F32),
            pltpu.VMEM((4, CHUNK, 2 * CHUNK), BF16),
            pltpu.VMEM((1, 128), F32),
            pltpu.VMEM((K_MAX, SUB, PIX), BF16),
            pltpu.VMEM((K_MAX, 2 * VB, PIX), BF16),
            pltpu.VMEM((2, SUB, H), F32),
            pltpu.VMEM((4, SUB, 2 * VB), BF16),
            pltpu.VMEM((NX, 4, SUB, 2 * VB), BF16),
            pltpu.VMEM((NZ, 2, SUB, 2 * VB), BF16),
            pltpu.VMEM((NZ, 2, SUB, 2 * VB), BF16),
            pltpu.VMEM((PIX, K_MAX * SUB), BF16),
            pltpu.VMEM((K_MAX * SUB, PIX), BF16),
            pltpu.SMEM(profile_index.shape, jnp.int32),
            pltpu.SMEM(group_power.shape, F32),
            pltpu.SMEM(group_slot.shape, jnp.int32),
            pltpu.SMEM(source_shift.shape, jnp.int32),
            pltpu.SMEM(slot_sub.shape, jnp.int32),
            pltpu.SMEM(tile_count.shape, jnp.int32),
            dma((12,)),
            dma((4, NX)),
            dma((NX, 4)),
            dma((NZ,)),
            dma((NZ,)),
        ],
        compiler_params=pltpu.CompilerParams(collective_id=0, has_side_effects=True),
    )(
        field_start,
        phase_table,
        profile_index,
        group_power,
        group_slot,
        source_shift,
        slot_sub,
        tile_count,
        row_weights,
        col_weights,
        jnp.asarray(propagator_blocks()),
        jnp.asarray(absorber_tail()),
    )


def solution(mesh):
    return jax.shard_map(
        per_device,
        mesh=mesh,
        in_specs=(
            P(None, "radial", None),
            P(),
            P(),
            P(),
            P(),
            P("range", None),
            P("range", None, None),
            P("range", None),
            P("range", "radial", None, None, None),
            P("range", "radial", None, None, None),
        ),
        out_specs=P("range", "radial", None, None),
        check_vma=False,
    )
```

time: 246 us -> 27.5 us (0.11)
  waiting for transfers between devices: 148 us -> 0 us
  other arithmetic: 29.2 us -> 0 us
  Pallas kernels: 0 us -> 22.9 us
  starting transfers between devices: 17.4 us -> 0 us
  local copies, waits for them, and re-layouts: 18.6 us -> 4.39 us
  between operations: 14.1 us -> 0.01 us
  matrix products: 11.8 us -> 0 us
  loops' own time: 6.04 us -> 0 us
    all_gather x1 -> x0, waiting for transfers between devices: 79.5 us -> none  [per_device(): every_block = lax.all_gather(polar, 'radial', axis=0, tiled=True)]
    ppermute x9 -> x0, waiting for transfers between devices: 68.8 us -> none  [passed_along(): lax.ppermute(value, axis, [(source, source + steps) for source in range(l...]
    dynamic_update_slice x10 -> x0, other arithmetic: 25.5 us -> none  [the longest x8 25.5 us: dft_tables(): lax.map(table_block, jnp.arange(8, dtype=jnp.int32))]
    pallas_call x0 -> x1, Pallas kernels: none -> 22.9 us  [per_device(): pl.pallas_call(kernel, out_shape=jax.ShapeDtypeStruct((1, 1, PIX, PIX), F...]
    ppermute x9 -> x0, starting transfers between devices: 17.3 us -> none  [passed_along(): lax.ppermute(value, axis, [(source, source + steps) for source in range(l...]
    dot_general x17 -> x0, matrix products: 11.8 us -> none  [the longest x4 5.42 us: march_slab(): jnp.dot(screened, cosine_table, preferred_element_type=jnp.float32)]
    another operation x11 -> x0, loops' own time: 6.04 us -> none  [the longest x1 5.51 us: dft_tables(): lax.map(table_block, jnp.arange(8, dtype=jnp.int32))]
    dynamic_slice x11 -> x0, local copies, waits for them, and re-layouts: 5.95 us -> none  [the longest x8 5.17 us: dft_tables(): lax.map(table_block, jnp.arange(8, dtype=jnp.int32))]
  transfers between devices with their start and end apart: 10 -> 0, of which waited for: 10 -> 0; matrix products, arithmetic and copies ran while one was open for 1% -> 0% of each run, Pallas kernels for 0% -> 0%
where the time goes in v1:
time: 27.5 us; the launch traced here: 27.3 us
  Pallas kernels  22.9 us (83%)
  local copies, waits for them, and re-layouts  4.39 us (16%)
    pallas_call x1, Pallas kernels, per_device(): pl.pallas_call(kernel, out_shape=jax.ShapeDtypeStruct((1, 1, PIX, PIX), F...  22.9 us
    unnamed x3, local copies, waits for them, and re-layouts  4.39 us

profile of v1, /device:TPU:24, one launch (start us, length us, event | category | flops | bytes accessed | tf_op | source)
XLA Modules:
  0.0 27.3 jit_solution(16030195902840281185)
XLA Ops:
  0.0 1.3 %copy.13.profile_hbm = s32[8,2]{1,0:T(8,128)} copy(s32[8,2]{0,1:T(2,128)} %param.14) | data formatting | bytes 128 | tf_op args[2]
  1.3 1.4 %copy.14.sub_hbm = s32[1,32,16]{2,1,0:T(8,128)} copy(s32[1,32,16]{1,2,0:T(8,128)} %param.18) | data formatting | bytes 4096 | tf_op args[6]
  2.7 22.9 %shard_map.118 = f32[1,1,256,256]{3,2,1,0:T(8,128)} custom-call(bf16[2,64,1024]{2,1,0:T(8,128)(2,1)} %field_hbm.1, f32[16,1024]{1,0:T(8,128)} %phase_hbm.1, s32[8,2]{1,0:T(8,128)} %copy.13.profile_hbm, f32[4]{0:T(128)} %power_hbm.1, s32[4]{0:T(128)} %slot_hbm.1, s32[1,32]{1,0:T(1,128)} %shift_hbm.1, s32[1,32,16]{2,1,0:T(8,128)} %copy.14.sub_hbm, ...), custom_call_target="tpu_custom_call" | custom-call | tf_op jit(solution)/shard_map/pallas_call | solution.py:320
  25.7 1.7 %copy.16 = f32[1,1,256,256]{3,2,1,0:T(8,128)} copy(f32[1,1,256,256]{3,2,1,0:T(8,128)} %shard_map.118) | data formatting | bytes 524288

commit v2 on v1

--- a/solution.py
+++ b/solution.py
@@ -145,7 +145,7 @@
     gain = power[slot[x_own // (GROUP_DEVICES // NZ)]]
 
     def one_step(re, im, number, step):
-        row = profile[number, step]
+        row = profile[step, number]
         cosine = cos_tab[pl.ds(row, 1), :]
         sine = sin_tab[pl.ds(row, 1), :]
         sr = re * cosine - im * sine
@@ -270,7 +270,7 @@
         source = lax.rem(lax.rem(begin + ahead, NX * NZ) // NZ, NX)
         for i in range(2):
             k = 2 * ahead + i
-            block = gathered[source, sub_of[0, tile, k]]
+            block = gathered[source, sub_of[0, k, tile]]
             block = jnp.where(k < count[0, tile], block, jnp.zeros_like(block))
             if dz:
                 picked[dz, i] = block
@@ -319,7 +319,7 @@
     anywhere = pl.BlockSpec(memory_space=pl.ANY)
     return pl.pallas_call(
         kernel,
-        out_shape=jax.ShapeDtypeStruct((1, 1, PIX, PIX), F32),
+        out_shape=pltpu.VMEM((1, 1, PIX, PIX), F32),
         in_specs=[anywhere] * 12,
         out_specs=pl.BlockSpec(memory_space=pltpu.VMEM),
         scratch_shapes=[
@@ -338,11 +338,11 @@
             pltpu.VMEM((NZ, 2, SUB, 2 * VB), BF16),
             pltpu.VMEM((PIX, K_MAX * SUB), BF16),
             pltpu.VMEM((K_MAX * SUB, PIX), BF16),
-            pltpu.SMEM(profile_index.shape, jnp.int32),
+            pltpu.SMEM(profile_index.shape[::-1], jnp.int32),
             pltpu.SMEM(group_power.shape, F32),
             pltpu.SMEM(group_slot.shape, jnp.int32),
             pltpu.SMEM(source_shift.shape, jnp.int32),
-            pltpu.SMEM(slot_sub.shape, jnp.int32),
+            pltpu.SMEM((1, K_MAX, NX * NZ), jnp.int32),
             pltpu.SMEM(tile_count.shape, jnp.int32),
             dma((12,)),
             dma((4, NX)),
@@ -354,11 +354,11 @@
     )(
         field_start,
         phase_table,
-        profile_index,
+        profile_index.T,
         group_power,
         group_slot,
         source_shift,
-        slot_sub,
+        slot_sub.transpose(0, 2, 1),
         tile_count,
         row_weights,
         col_weights,

time: 27.5 us -> 23 us (0.84)
  local copies, waits for them, and re-layouts: 4.39 us -> 0.71 us
  Pallas kernels: 22.9 us -> 22.2 us
    unnamed x3 -> x1, local copies, waits for them, and re-layouts: 4.39 us -> 0.71 us
    pallas_call x1, Pallas kernels: 22.9 us -> 22.2 us  [per_device(): pl.pallas_call(kernel, out_shape=pltpu.VMEM((1, 1, PIX, PIX), F32), in_sp...]
where the time goes in v2:
time: 23 us
  Pallas kernels  22.2 us (97%)
  local copies, waits for them, and re-layouts  0.71 us (3%)
    pallas_call x1, Pallas kernels, per_device(): pl.pallas_call(kernel, out_shape=pltpu.VMEM((1, 1, PIX, PIX), F32), in_sp...  22.2 us
    unnamed x1, local copies, waits for them, and re-layouts  0.71 us

profile of v2, /device:TPU:24, one launch (start us, length us, event | category | flops | bytes accessed | tf_op | source)
XLA Modules:
  0.0 23.0 jit_solution(2233764389681781880)
XLA Ops:
  0.0 22.2 %shard_map.118 = f32[1,1,256,256]{3,2,1,0:T(8,128)S(1)} custom-call(bf16[2,64,1024]{2,1,0:T(8,128)(2,1)} %field_hbm.1, f32[16,1024]{1,0:T(8,128)} %phase_hbm.1, s32[2,8]{1,0:T(2,128)} %bitcast.3, f32[4]{0:T(128)} %power_hbm.1, s32[4]{0:T(128)} %slot_hbm.1, s32[1,32]{1,0:T(1,128)} %shift_hbm.1, s32[1,16,32]{2,1,0:T(8,128)} %bitcast.2, s32[1,32]{1,0:T(1,128)} %count_hbm.1, ...), custom_call_target="tpu_custom_call" | custom-call | tf_op jit(solution)/shard_map/pallas_call | solution.py:320
  22.2 0.7 %copy.14 = f32[1,1,256,256]{3,2,1,0:T(8,128)} copy(f32[1,1,256,256]{3,2,1,0:T(8,128)S(1)} %shard_map.118) | data formatting | bytes 524288
